TPU v7x, 512 devices: a whole 4x4x16 slice. The times are simulated.
512 devices in a mesh: row: 16 (over z), col: 32 (over y, x, core).
Axes of the slice: x: 4, y: 4, z: 16, core: 2. Of those that a mesh axis runs over, the one named last changes fastest.
Arguments:
- right_side: bfloat16 [16384, 16384], P('row', 'col'), may hold values from -180 to 180
- theta_left: bfloat16 [512, 16384], P(None, 'row'), may hold values from -0.125 to 0.125
- theta_right: bfloat16 [512, 16384], P(None, 'col'), may hold values from -0.125 to 0.125
- query_rows: int32 [1024, 2], replicated, may hold values from 0 to 16384, as said below
- query_cols: int32 [1024, 2], replicated, may hold values from 0 to 16384, as said below
Outputs:
- residual: float32 [16384, 16384], P('row', 'col')
- step_ratio: float32 [1], replicated
- answers: float32 [1024], replicated
Inputs may be any that keep to these rules, and one draw needn't show every extreme that they name: `query_rows`: each row is a start and an end with 0 <= start < end <= 16384. `query_cols`: each row is a start and an end with 0 <= start < end <= 16384.
All inputs are finite; a program needn't handle non-finite values.
Results may differ from a plain program's by a relative error of at most 0.0003.
Values sent between devices are 32-bit elements; how exact they have to be, the bound alone decides.
A program may use at most 64 MiB of HBM per device.

v0:
```python
import jax
import jax.numpy as jnp
from jax import lax
from jax.sharding import PartitionSpec as P


def prefix_2(part, axis, combine, identity):
    place = lax.axis_index(axis)
    gathered = lax.all_gather(part, axis)
    state = jnp.zeros_like(part) + jnp.asarray(identity, part.dtype)

    def one(hop, state):
        return combine(state, lax.dynamic_index_in_dim(gathered, hop, 0, False))

    return lax.fori_loop(0, place, one, state)


def add_pair(earlier, later):
    return earlier + later


def cum_last(values):
    length = values.shape[1]
    block_len = 128
    index_line = jnp.arange(block_len)
    upper_tri = (index_line[:, None] <= index_line[None, :]).astype(jnp.float32)
    pieces = values.reshape(values.shape[0], length // block_len, block_len)
    within = jnp.einsum("rbk,kj->rbj", pieces, upper_tri, precision=lax.Precision.HIGHEST)
    totals = within[:, :, -1]
    carried = jnp.cumsum(totals, axis=1) - totals
    return (within + carried[:, :, None]).reshape(values.shape)


def cum_first(values):
    length = values.shape[0]
    block_len = 128
    index_line = jnp.arange(block_len)
    lower_tri = (index_line[:, None] >= index_line[None, :]).astype(jnp.float32)
    pieces = values.reshape(length // block_len, block_len, values.shape[1])
    within = jnp.einsum("ik,bkc->bic", lower_tri, pieces, precision=lax.Precision.HIGHEST)
    totals = within[:, -1, :]
    carried = jnp.cumsum(totals, axis=0) - totals
    return (within + carried[:, None, :]).reshape(values.shape)


def down_scan(column_totals):
    return prefix_2(column_totals, "row", add_pair, jnp.zeros_like(column_totals))


def shards(right_side, theta_left, theta_right, query_rows, query_cols):
    highest = lax.Precision.HIGHEST
    block_rows, block_cols = right_side.shape
    start_field = right_side.astype(jnp.float32)
    left_wide = theta_left.astype(jnp.float32)
    right_wide = theta_right.astype(jnp.float32)
    start_norm = lax.psum(jnp.sum(start_field * start_field), ("row", "col"))
    partial_right = lax.dot_general(
        right_side, theta_right, (((1,), (1,)), ((), ())), preferred_element_type=jnp.float32
    )
    summed_right = lax.psum(partial_right, "col")
    middle = start_field + jnp.dot(
        summed_right, right_wide, precision=highest, preferred_element_type=jnp.float32
    )
    partial_left = jnp.dot(left_wide, middle, precision=highest, preferred_element_type=jnp.float32)
    summed_left = lax.psum(partial_left, "row")
    image_field = middle + lax.dot_general(
        left_wide,
        summed_left,
        (((0,), (0,)), ((), ())),
        precision=highest,
        preferred_element_type=jnp.float32,
    )
    curvature = lax.psum(jnp.sum(start_field * image_field), ("row", "col"))
    alpha_step = start_norm / curvature
    residual = start_field - alpha_step * image_field
    fresh = lax.psum(jnp.sum(residual * residual), ("row", "col"))
    step_ratio = (fresh / start_norm).reshape(1)
    solution = alpha_step * start_field
    across = cum_last(solution)
    row_totals = across[:, -1]
    left_carry = prefix_2(row_totals, "col", add_pair, jnp.zeros_like(row_totals))
    vertical = cum_first(across + left_carry[:, None])
    upper_carry = down_scan(vertical[-1, :])
    prefix = vertical + upper_carry[None, :]
    row_start = lax.axis_index("row") * block_rows
    col_start = lax.axis_index("col") * block_cols
    flat_prefix = prefix.reshape(-1)

    def corner_value(row_bound, col_bound):
        local_row = row_bound - 1 - row_start
        local_col = col_bound - 1 - col_start
        inside = (
            (local_row >= 0)
            & (local_row < block_rows)
            & (local_col >= 0)
            & (local_col < block_cols)
        )
        position_flat = jnp.clip(local_row, 0, block_rows - 1) * block_cols + jnp.clip(
            local_col, 0, block_cols - 1
        )
        return jnp.where(inside, jnp.take(flat_prefix, position_flat), 0.0)

    low_row = query_rows[:, 0]
    high_row = query_rows[:, 1]
    low_col = query_cols[:, 0]
    high_col = query_cols[:, 1]
    partial_answers = (
        corner_value(high_row, high_col)
        - corner_value(low_row, high_col)
        - corner_value(high_row, low_col)
        + corner_value(low_row, low_col)
    )
    combined = lax.psum(partial_answers, ("row", "col"))
    area = (high_row - low_row).astype(jnp.float32) * (high_col - low_col).astype(jnp.float32)
    answers = combined / jnp.sqrt(area)
    return (residual, step_ratio, answers)


def solution(mesh):
    return jax.shard_map(
        shards,
        mesh=mesh,
        in_specs=(P("row", "col"), P(None, "row"), P(None, "col"), P(), P()),
        out_specs=(P("row", "col"), P(), P()),
        check_vma=False,
    )
```

profile of v0, /device:TPU:1, one launch (start us, length us, event | category | flops | bytes accessed | tf_op | source)
XLA Modules:
  0.0 611.5 jit_solution(15123079067743380518)
XLA Ops:
  7.2 0.0 copy-start
  7.2 0.0 copy-start.1
  7.2 0.0 copy-start.2
  7.2 0.0 all-reduce.5.cloned.1.call-start
  7.2 3.5 fusion.25
  10.7 0.0 all-reduce.5.cloned.1.call-update
  10.8 0.0 all-reduce.7.cloned.1.call-start
  10.8 0.0 copy-done.1
  10.8 0.0 copy-done.2
  10.9 144.4 %all-reduce.5.cloned.1.call-done = f32[1024,512]{1,0:T(8,128)} async-done(((f32[1024,512]{1,0:T(8,128)}), f32[1024,512]{1,0:T(8,128)}) %all-reduce.5.cloned.1.call-update) | async-done | bytes 2097168 | tf_op jit(solution)/shard_map/psum | solution.py:60
  155.3 3.8 convert_add_fusion
  159.1 0.0 copy-done
  159.2 4.4 convolution_bitcast_fusion
  163.6 0.0 all-reduce.7.cloned.1.call-update
  163.6 0.6 fusion.21
  164.2 0.7 and_reduce_fusion.3
  164.9 0.6 fusion.22
  165.5 0.6 fusion.23
  166.1 0.6 fusion.24
  166.7 0.6 multiply_rsqrt_fusion
  167.3 125.6 %all-reduce.7.cloned.1.call-done = f32[512,512]{0,1:T(8,128)} async-done(((f32[512,512]{0,1:T(8,128)}), f32[512,512]{0,1:T(8,128)}) %all-reduce.7.cloned.1.call-update) | async-done | bytes 1048592 | tf_op jit(solution)/shard_map/psum | solution.py:65
  292.9 5.5 fusion.1
  298.4 110.7 %all-reduce.1 = (f32[]{:T(128)}, f32[]{:T(128)}) all-reduce(f32[]{:T(128)} %get-tuple-element.53, f32[]{:T(128)} %get-tuple-element.52), channel_id=1, replica_groups=mesh['row'=16,'col'=32] {'row','col'}, use_global_device_ids=true, to_apply=%region_1.0 | all-reduce | flops 2 | bytes 16 | tf_op jit(solution)/shard_map/psum | solution.py:56
  410.4 4.5 multiply_reduce_fusion
  414.9 1.2 fusion.3
  416.2 0.3 broadcast_add_fusion.1
  416.5 24.4 %all-gather = f32[32768,1]{0,1:T(1,128)S(1)} all-gather(f32[1024,1]{0,1:T(1,128)S(1)} %slice.41), channel_id=2, replica_groups=mesh['row'=16,'col'=32] {'col'}, dimensions={0}, use_global_device_ids=true | all-gather | bytes 135168 | tf_op jit(solution)/shard_map/all_gather | solution.py:9
  440.9 0.5 broadcast.172
  441.5 0.9 reduce.11
  442.4 0.1 while.20
  442.4 1.8 copy.22
  444.3 1.9 copy.16
  446.2 1.4 fusion.8
  447.7 0.2 broadcast_add_fusion
  447.9 19.9 %all-gather.1 = f32[16,1,512]{2,1,0:T(1,128)S(1)} all-gather(f32[1,1,512]{2,1,0:T(1,128)S(1)} %slice_bitcast_fusion), channel_id=1, replica_groups=mesh['row'=16,'col'=32] {'row'}, dimensions={0}, use_global_device_ids=true | all-gather | bytes 34816 | tf_op jit(solution)/shard_map/all_gather | solution.py:9
  467.9 0.3 broadcast_bitcast_fusion
  468.1 0.5 copy.24
  468.7 0.5 copy.23
  469.2 0.0 copy-start.4
  469.2 0.2 add.122
  469.5 0.5 copy-done.4
  469.9 0.0 copy-start.7
  469.9 6.1 %gather_fusion = f32[1024]{0:T(1024)S(1)} fusion(f32[524288]{0:T(1024)S(1)} %add.122, s32[1024]{0:T(1024)S(1)} %copy-done.4), kind=kCustom, calls=%fused_computation.clone | custom fusion | bytes 12288 | tf_op jit(solution)/shard_map/jit(_take)/gather | solution.py:101
  476.1 0.0 copy-done.7
  476.1 0.0 copy-start.5
  476.1 6.2 %gather_fusion.1 = f32[1024]{0:T(1024)S(1)} fusion(f32[524288]{0:T(1024)S(1)} %add.122, s32[1024]{0:T(1024)S(1)} %copy-done.7), kind=kCustom, calls=%fused_computation.1.clone | custom fusion | bytes 12288 | tf_op jit(solution)/shard_map/jit(_take)/gather | solution.py:101
  482.2 0.0 copy-done.5
  482.3 0.0 copy-start.6
  482.3 6.2 %gather_fusion.2 = f32[1024]{0:T(1024)S(1)} fusion(f32[524288]{0:T(1024)S(1)} %add.122, s32[1024]{0:T(1024)S(1)} %copy-done.5), kind=kCustom, calls=%fused_computation.2.clone | custom fusion | bytes 12288 | tf_op jit(solution)/shard_map/jit(_take)/gather | solution.py:101
  488.4 0.0 copy-done.6
  488.4 0.0 copy-start.8
  488.5 0.0 copy-start.9
  488.5 0.0 copy-start.10
  488.5 0.0 copy-start.11
  488.5 0.0 copy-start.3
  488.5 6.2 %gather_fusion.3 = f32[1024]{0:T(1024)S(1)} fusion(f32[524288]{0:T(1024)S(1)} %add.122, s32[1024]{0:T(1024)S(1)} %copy-done.6), kind=kCustom, calls=%fused_computation.3.clone | custom fusion | bytes 12288 | tf_op jit(solution)/shard_map/jit(_take)/gather | solution.py:101
  494.7 0.0 copy-done.8
  494.7 0.0 copy-done.9
  494.7 0.0 copy-done.10
  494.7 0.0 copy-done.11
  494.7 106.9 %all-reduce = (f32[]{:T(128)}, f32[1024]{0:T(1024)S(1)}) all-reduce(f32[]{:T(128)} %get-tuple-element.78, f32[1024]{0:T(1024)S(1)} %fusion.18), channel_id=1, replica_groups=mesh['row'=16,'col'=32] {'row','col'}, use_global_device_ids=true, to_apply=%region_7.0 | all-reduce | flops 1025 | bytes 8200 | tf_op jit(solution)/shard_map/psum | solution.py:76
  602.9 0.0 copy-done.3
  602.9 0.6 div.11
  (15 shorter events, 0.2 us)
Async XLA Ops:
  7.2 152.0 %copy-start = (bf16[512,1024]{1,0:T(8,128)(2,1)S(1)}, bf16[512,1024]{1,0:T(8,128)(2,1)}, u32[]{:S(2)}) copy-start(bf16[512,1024]{1,0:T(8,128)(2,1)} %param.12) | copy-start | bytes 3145732
  7.2 3.6 copy-start.1
  7.2 3.6 copy-start.2
  7.2 148.1 %all-reduce.5.cloned.1.call-start = ((), (), s32[]{:S(2)}) async-start(), calls=%async_computation | async-start | bytes 4194304 | tf_op jit(solution)/shard_map/psum | solution.py:60
  10.8 282.2 %all-reduce.7.cloned.1.call-start = ((), (), s32[]{:S(2)}) async-start(), calls=%async_computation.1 | async-start | bytes 2097152 | tf_op jit(solution)/shard_map/psum | solution.py:65
  469.2 0.7 copy-start.4
  469.9 6.2 %copy-start.7 = (s32[1024]{0:T(1024)S(1)}, s32[1024]{0:T(1024)}, u32[]{:S(2)}) copy-start(s32[1024]{0:T(1024)} %fusion.22) | copy-start | bytes 12292
  476.1 6.2 %copy-start.5 = (s32[1024]{0:T(1024)S(1)}, s32[1024]{0:T(1024)}, u32[]{:S(2)}) copy-start(s32[1024]{0:T(1024)} %fusion.23) | copy-start | bytes 12292
  482.3 6.2 %copy-start.6 = (s32[1024]{0:T(1024)S(1)}, s32[1024]{0:T(1024)}, u32[]{:S(2)}) copy-start(s32[1024]{0:T(1024)} %fusion.24) | copy-start | bytes 12292
  488.4 6.2 %copy-start.8 = (pred[1024]{0:T(1024)(128)(4,1)S(1)}, pred[1024]{0:T(1024)(128)(4,1)}, u32[]{:S(2)}) copy-start(pred[1024]{0:T(1024)(128)(4,1)} %get-tuple-element.54) | copy-start | bytes 3076
  488.5 6.2 %copy-start.9 = (pred[1024]{0:T(1024)(128)(4,1)S(1)}, pred[1024]{0:T(1024)(128)(4,1)}, u32[]{:S(2)}) copy-start(pred[1024]{0:T(1024)(128)(4,1)} %get-tuple-element.55) | copy-start | bytes 3076
  488.5 6.2 %copy-start.10 = (pred[1024]{0:T(1024)(128)(4,1)S(1)}, pred[1024]{0:T(1024)(128)(4,1)}, u32[]{:S(2)}) copy-start(pred[1024]{0:T(1024)(128)(4,1)} %get-tuple-element.56) | copy-start | bytes 3076
  488.5 6.2 %copy-start.11 = (pred[1024]{0:T(1024)(128)(4,1)S(1)}, pred[1024]{0:T(1024)(128)(4,1)}, u32[]{:S(2)}) copy-start(pred[1024]{0:T(1024)(128)(4,1)} %get-tuple-element.57) | copy-start | bytes 3076
  488.5 114.4 %copy-start.3 = (f32[1024,1]{0,1:T(1,128)S(1)}, f32[1024,1]{0,1:T(1,128)}, u32[]{:S(2)}) copy-start(f32[1024,1]{0,1:T(1,128)} %multiply_rsqrt_fusion) | copy-start | bytes 12292
Sparse Core Ops, SparseCore 0:
  11.9 143.3 all-reduce.4
  163.7 129.1 all-reduce.6
where the time goes:
time: 612 us
  waiting for transfers between devices  270 us (44%)
  blocking collectives  262 us (43%)
  local copies, waits for them, and re-layouts  30.8 us (5%)
  matrix products  19.9 us (3%)
  between operations  18.2 us (3%)
  other arithmetic  10.5 us (2%)
    psum x1, waiting for transfers between devices, shards(): summed_right = lax.psum(partial_right, 'col')  144 us
    psum x1, waiting for transfers between devices, shards(): summed_left = lax.psum(partial_left, 'row')  126 us
    psum x1, blocking collectives, shards(): start_norm = lax.psum(jnp.sum(start_field * start_field), ('row', 'col'))  111 us
    psum x1, blocking collectives, shards(): fresh = lax.psum(jnp.sum(residual * residual), ('row', 'col'))  107 us
    all_gather x2, blocking collectives, prefix_2(): gathered = lax.all_gather(part, axis)  44.4 us
    gather x4, local copies, waits for them, and re-layouts, corner_value(): return jnp.where(inside, jnp.take(flat_prefix, position_flat), 0.0)  24.6 us
  transfers between devices with their start and end apart: 2, of which 2 were waited for; matrix products, arithmetic and copies ran while one was open for 1% of the time, Pallas kernels for 0%

commit v1 on v0

v1 whole, which is shorter than its diff:
```python
import functools

import jax
import jax.numpy as jnp
from jax import lax
from jax.experimental import pallas as pl
from jax.experimental.pallas import tpu as pltpu
from jax.sharding import PartitionSpec as P

MESH = pl.DeviceIdType.MESH
F32, BF16 = jnp.float32, jnp.bfloat16
NZ, NX, NY = 16, 4, 4
ROWS, COLS, Q, NQ = 1024, 512, 512, 1024
NSUB = 2
SUBW = COLS // NSUB
MSG = NQ + 256
NT = (((1,), (1,)), ((), ()))


def dot(a, b):
    return jnp.dot(a, b, preferred_element_type=F32)


def split(value):
    high = value.astype(BF16)
    return high, (value - high.astype(F32)).astype(BF16)


def dot_split(value, b):
    high, low = split(value)
    return dot(high, b) + dot(low, b)


def copy_to(src, dst, send, recv, device):
    return pltpu.make_async_remote_copy(
        src_ref=src, dst_ref=dst, send_sem=send, recv_sem=recv, device_id=device, device_id_type=MESH
    )


def kernel(
    v_ref, l_ref, r_ref, qr_ref, qc_ref,
    out_ref, ans_ref, ratio_ref,
    lt, bt, sp, sp_in, rs_in, s_full, tp, t_right, t_left, t_full, u_out, u_in, u_all, u_tile, u_full,
    x1, resid, z_hi, z_lo, m_own, m_z, m_plane, m_pair, e_own, e_z, e_plane, e_pair,
    pair_s, pair_r, one_s, one_r, fwd_s, fwd_r, tr_s, tr_r, tl_s, tl_r, gr_s, gr_r, gl_s, gl_r, out_sem,
):
    z = lax.axis_index("row")
    c = lax.axis_index("col")
    core = lax.rem(c, 2)
    chip = c // 2
    xx = lax.rem(chip, NX)
    yy = chip // NX

    def z_peer(d):
        return (lax.rem(z + d, NZ), c)

    def plane_chip(j):
        return lax.rem(yy + j // NX, NY) * NX + lax.rem(xx + lax.rem(j, NX), NX)

    def plane_peer(j):
        return (z, plane_chip(j) * 2 + core)

    other = (z, chip * 2 + 1 - core)
    right, left = z_peer(1), z_peer(NZ - 1)

    barrier = pltpu.get_barrier_semaphore()

    def greet(d, carry):
        pl.semaphore_signal(barrier, inc=1, device_id=z_peer(d), device_id_type=MESH)
        pl.semaphore_signal(barrier, inc=1, device_id=plane_peer(d), device_id_type=MESH)
        return carry

    pl.semaphore_signal(barrier, inc=1, device_id=other, device_id_type=MESH)
    lax.fori_loop(1, NZ, greet, 0)

    def s_half(half):
        def tile(i, carry):
            at = pl.multiple_of(half * 256 + i * 128, 128)
            sp[pl.ds(at, 128), :] = lax.dot_general(
                r_ref[pl.ds(at, 128), :], v_ref[...], NT, preferred_element_type=F32
            )
            return carry

        lax.fori_loop(0, 2, tile, 0)

    def t_tile(i, carry):
        at = pl.multiple_of(i * 128, 128)
        tp[pl.ds(at, 128), :] = dot(l_ref[pl.ds(at, 128), :], v_ref[...])
        return carry

    s_half(1 - core)
    lax.fori_loop(0, 4, t_tile, 0)
    pl.semaphore_wait(barrier, 31)

    give = (1 - core) * 256
    keep = core * 256

    def chunk_rows(base, d):
        return pl.ds(pl.multiple_of(base + lax.rem(yy + d, NY) * 64, 64), 64)

    def pair_copy(d):
        return copy_to(
            sp.at[chunk_rows(give, d)], sp_in.at[chunk_rows(0, d)], pair_s.at[d], pair_r.at[d], other
        )

    for d in (1, 2, 3, 0):
        pair_copy(d).start()

    def t_rows(block):
        return pl.ds(pl.multiple_of(lax.rem(block + 2 * NZ, NZ) * 32, 32), 32)

    def sub(h):
        return pl.ds(h * SUBW, SUBW)

    def t_rs(s):
        for h in range(NSUB):
            if s <= 7:
                rows = t_rows(z + 8 - s)
                if s == 1:
                    src = tp.at[rows, sub(h)]
                else:
                    src = t_right.at[s - 2, :, sub(h)]
                    copy_to(src, src, tr_s.at[s - 2, h], tr_r.at[s - 2, h], right).wait_recv()
                    t_right[s - 2, :, sub(h)] = t_right[s - 2, :, sub(h)] + tp[rows, sub(h)]
                copy_to(src, t_right.at[s - 1, :, sub(h)], tr_s.at[s - 1, h], tr_r.at[s - 1, h], right).start()
            rows = t_rows(z - 9 + s)
            if s == 1:
                src = tp.at[rows, sub(h)]
            else:
                src = t_left.at[s - 2, :, sub(h)]
                copy_to(src, src, tl_s.at[s - 2, h], tl_r.at[s - 2, h], left).wait_recv()
                t_left[s - 2, :, sub(h)] = t_left[s - 2, :, sub(h)] + tp[rows, sub(h)]
            copy_to(src, t_left.at[s - 1, :, sub(h)], tl_s.at[s - 1, h], tl_r.at[s - 1, h], left).start()

    def t_own():
        rows = t_rows(z)
        total = jnp.zeros((1, SUBW), F32)
        for h in range(NSUB):
            a, b = t_right.at[6, :, sub(h)], t_left.at[7, :, sub(h)]
            copy_to(a, a, tr_s.at[6, h], tr_r.at[6, h], right).wait_recv()
            copy_to(b, b, tl_s.at[7, h], tl_r.at[7, h], left).wait_recv()
            block = tp[rows, sub(h)] + t_right[6, :, sub(h)] + t_left[7, :, sub(h)]
            t_full[rows, sub(h)] = block
            total = total + jnp.sum(block * block, axis=0, keepdims=True)
        return jnp.sum(total)

    def t_ag(s):
        for h in range(NSUB):
            if s <= 8:
                if s <= 7:
                    here = t_full.at[t_rows(z - s + 1), sub(h)]
                    if s > 1:
                        copy_to(here, here, gr_s.at[s - 2, h], gr_r.at[s - 2, h], right).wait_recv()
                    copy_to(here, here, gr_s.at[s - 1, h], gr_r.at[s - 1, h], right).start()
                here = t_full.at[t_rows(z + s - 1), sub(h)]
                if s > 1:
                    copy_to(here, here, gl_s.at[s - 2, h], gl_r.at[s - 2, h], left).wait_recv()
                copy_to(here, here, gl_s.at[s - 1, h], gl_r.at[s - 1, h], left).start()
            else:
                here = t_full.at[t_rows(z - 7), sub(h)]
                copy_to(here, here, gr_s.at[6, h], gr_r.at[6, h], right).wait_recv()
                here = t_full.at[t_rows(z + 8), sub(h)]
                copy_to(here, here, gl_s.at[7, h], gl_r.at[7, h], left).wait_recv()

    t_rs(1)
    s_half(core)

    def plane_copy(j):
        rows = pl.ds(pl.multiple_of(keep + plane_chip(j) * 16, 16), 16)
        return copy_to(sp.at[rows], rs_in.at[j - 1], one_s.at[0], one_r.at[0], plane_peer(j))

    for d in (1, 2, 3, 0):
        pair_copy(d).wait_recv()
        mine, got = chunk_rows(keep, d), chunk_rows(0, d)
        sp[mine, :] = sp[mine, :] + sp_in[got, :]

        def send(j, carry):
            plane_copy(j).start()
            return carry

        lax.fori_loop(4 * d if d else 1, 4 * d + 4, send, 0)

    t_rs(2)

    def lt_tile(i, carry):
        at = pl.multiple_of(i * 128, 128)
        lt[pl.ds(at, 128), :] = l_ref[:, pl.ds(at, 128)].astype(F32).T.astype(BF16)
        return carry

    lax.fori_loop(0, 4, lt_tile, 0)
    t_rs(3)
    lax.fori_loop(4, 8, lt_tile, 0)

    def bt_tile(i, carry):
        at = pl.multiple_of(i * 128, 128)
        index = lax.broadcasted_iota(jnp.int32, (128, NQ), 0) + (at + c * COLS)
        inside = (index >= qc_ref[0:1, :]) & (index < qc_ref[1:2, :])
        bt[pl.ds(at, 128), :] = jnp.where(inside, 1.0, 0.0).astype(BF16)
        return carry

    lax.fori_loop(0, 4, bt_tile, 0)
    t_rs(4)

    def answer_tile(i, carry):
        total, norm = carry
        at = pl.multiple_of(i * 128, 128)
        block = v_ref[pl.ds(at, 128), :]
        across = dot(block, bt[...])
        index = lax.broadcasted_iota(jnp.int32, (128, NQ), 0) + (at + z * ROWS)
        inside = (index >= qr_ref[0:1, :]) & (index < qr_ref[1:2, :])
        total = total + jnp.sum(jnp.where(inside, across, 0.0), axis=0, keepdims=True)
        wide = block.astype(F32)
        norm = norm + jnp.sum(wide * wide, axis=0, keepdims=True)
        return total, norm

    carry = (jnp.zeros((1, NQ), F32), jnp.zeros((1, COLS), F32))
    carry = lax.fori_loop(0, 3, answer_tile, carry)
    t_rs(5)
    carry = lax.fori_loop(3, 6, answer_tile, carry)
    t_rs(6)
    carry = lax.fori_loop(6, 8, answer_tile, carry)
    m_own[:, 0:NQ] = carry[0]
    m_own[:, NQ : NQ + 128] = jnp.broadcast_to(jnp.sum(carry[1]), (1, 128))

    copy_to(rs_in, rs_in, one_s.at[0], one_r.at[0], other).wait_recv()
    own_rows = pl.ds(pl.multiple_of(keep + chip * 16, 16), 16)

    def add_in(j, total):
        return total + rs_in[j]

    s_block = lax.fori_loop(0, 15, add_in, sp[own_rows, :])
    s_full[own_rows, :] = s_block

    def s_copy(j):
        here = s_full.at[own_rows]
        return copy_to(here, here, one_s.at[1], one_r.at[1], plane_peer(j))

    def start_all(make):
        def one(j, carry):
            make(j).start()
            return carry

        lax.fori_loop(1, 16, one, 0)

    s_high, s_low = split(s_block)
    u_part = lax.dot_general(s_high, l_ref[...], NT, preferred_element_type=F32) + lax.dot_general(
        s_low, l_ref[...], NT, preferred_element_type=F32
    )
    for i in range(NZ):
        u_out[i] = u_part[i : i + 1, :]

    def u_copy(d):
        return copy_to(u_out.at[lax.rem(z + d, NZ)], u_in.at[d - 1], one_s.at[2], one_r.at[2], z_peer(d))

    start_all(u_copy)
    start_all(s_copy)
    rest = jnp.sum(s_block * s_block)
    t_rs(7)
    t_rs(8)
    rest = rest + t_own()
    t_ag(1)

    copy_to(u_in, u_in, one_s.at[2], one_r.at[2], other).wait_recv()

    def add_row(j, total):
        return total + u_in[j]

    u_row = lax.fori_loop(0, 15, add_row, u_out[z])
    u_all[z] = u_row

    def ug_copy(d):
        return copy_to(u_all.at[z], u_all.at[z], one_s.at[3], one_r.at[3], z_peer(d))

    start_all(ug_copy)
    rest = rest + jnp.sum(u_row * u_row)
    m_own[:, NQ + 128 :] = jnp.broadcast_to(rest, (1, 128))

    def m_copy(d):
        return copy_to(m_own, m_z.at[d - 1], one_s.at[4], one_r.at[4], z_peer(d))

    start_all(m_copy)
    t_ag(2)

    copy_to(s_full.at[0:240], s_full.at[0:240], one_s.at[1], one_r.at[1], other).wait_recv()
    kept = s_full.at[pl.ds(pl.multiple_of(keep, 256), 256)]
    given = s_full.at[pl.ds(pl.multiple_of(give, 256), 256)]
    copy_to(kept, kept, fwd_s.at[0], fwd_r.at[0], other).start()
    t_ag(3)

    copy_to(u_all.at[0:15], u_all.at[0:15], one_s.at[3], one_r.at[3], other).wait_recv()
    for i in range(NZ):
        u_tile[i : i + 1, :] = u_all[i]
    u_full[own_rows, :] = u_tile[...]

    def up_copy(j):
        here = u_full.at[own_rows]
        return copy_to(here, here, one_s.at[5], one_r.at[5], plane_peer(j))

    start_all(up_copy)

    copy_to(m_z, m_z, one_s.at[4], one_r.at[4], other).wait_recv()

    def add_m(buffer):
        return lambda j, total: total + buffer[j]

    m_plane[15] = lax.fori_loop(0, 15, add_m(m_z), m_own[...])

    def mp_copy(j):
        return copy_to(m_plane.at[15], m_plane.at[j - 1], one_s.at[6], one_r.at[6], plane_peer(j))

    start_all(mp_copy)
    t_ag(4)

    copy_to(given, given, fwd_s.at[0], fwd_r.at[0], other).wait_recv()

    def x_tile(i, carry):
        at = pl.multiple_of(i * 128, 128)
        high, low = split(s_full[:, pl.ds(at, 128)].T)
        x1[pl.ds(at, 128), :] = v_ref[pl.ds(at, 128), :].astype(F32) + dot(high, r_ref[...]) + dot(low, r_ref[...])
        return carry

    lax.fori_loop(0, 3, x_tile, 0)
    t_ag(5)
    lax.fori_loop(3, 6, x_tile, 0)
    t_ag(6)
    lax.fori_loop(6, 8, x_tile, 0)

    copy_to(u_full.at[0:240], u_full.at[0:240], one_s.at[5], one_r.at[5], other).wait_recv()
    u_kept = u_full.at[pl.ds(pl.multiple_of(keep, 256), 256)]
    u_given = u_full.at[pl.ds(pl.multiple_of(give, 256), 256)]
    copy_to(u_kept, u_kept, fwd_s.at[1], fwd_r.at[1], other).start()

    copy_to(m_plane.at[0:15], m_plane.at[0:15], one_s.at[6], one_r.at[6], other).wait_recv()
    m_pair[0] = lax.fori_loop(0, 16, add_m(m_plane), jnp.zeros((1, MSG), F32))
    copy_to(m_pair.at[0], m_pair.at[1], fwd_s.at[2], fwd_r.at[2], other).start()
    t_ag(7)
    t_ag(8)

    copy_to(m_pair.at[1], m_pair.at[1], fwd_s.at[2], fwd_r.at[2], other).wait_recv()
    message = m_pair[0] + m_pair[1]
    norm = message[:, NQ : NQ + 128]
    alpha = norm / (norm + message[:, NQ + 128 :])
    spans = (qr_ref[1:2, :] - qr_ref[0:1, :]).astype(F32) * (qc_ref[1:2, :] - qc_ref[0:1, :]).astype(F32)
    alpha = alpha[0:1, 0:1]
    ans_ref[...] = message[:, 0:NQ] * alpha / jnp.sqrt(spans)

    copy_to(u_given, u_given, fwd_s.at[1], fwd_r.at[1], other).wait_recv()
    t_ag(9)

    def z_tile(i, carry):
        at = pl.multiple_of(i * 128, 128)
        high, low = split(u_full[:, pl.ds(at, 128)].T)
        block = t_full[pl.ds(at, 128), :] + dot(high, r_ref[...]) + dot(low, r_ref[...])
        high, low = split(block)
        z_hi[pl.ds(at, 128), :] = high
        z_lo[pl.ds(at, 128), :] = low
        return carry

    lax.fori_loop(0, 4, z_tile, 0)

    def final_tile(i, total):
        at = pl.multiple_of(i * 128, 128)
        rows = lt[pl.ds(at, 128), :]
        image = x1[pl.ds(at, 128), :] + dot(rows, z_hi[...]) + dot(rows, z_lo[...])
        block = v_ref[pl.ds(at, 128), :].astype(F32) - alpha * image
        resid[pl.ds(at, 128), :] = block
        return total + jnp.sum(block * block, axis=0, keepdims=True)

    fresh = lax.fori_loop(0, 8, final_tile, jnp.zeros((1, COLS), F32))
    out_copy = pltpu.make_async_copy(resid, out_ref, out_sem)
    out_copy.start()

    e_own[...] = jnp.broadcast_to(jnp.sum(fresh), (1, 128))

    def ez_copy(d):
        return copy_to(e_own, e_z.at[d - 1], one_s.at[7], one_r.at[7], z_peer(d))

    start_all(ez_copy)
    copy_to(e_z, e_z, one_s.at[7], one_r.at[7], other).wait_recv()
    e_plane[15] = lax.fori_loop(0, 15, add_m(e_z), e_own[...])

    def ep_copy(j):
        return copy_to(e_plane.at[15], e_plane.at[j - 1], one_s.at[8], one_r.at[8], plane_peer(j))

    start_all(ep_copy)
    copy_to(e_plane.at[0:15], e_plane.at[0:15], one_s.at[8], one_r.at[8], other).wait_recv()
    e_pair[0] = lax.fori_loop(0, 16, add_m(e_plane), jnp.zeros((1, 128), F32))
    copy_to(e_pair.at[0], e_pair.at[1], fwd_s.at[3], fwd_r.at[3], other).start()
    copy_to(e_pair.at[1], e_pair.at[1], fwd_s.at[3], fwd_r.at[3], other).wait_recv()
    ratio_ref[...] = (e_pair[0] + e_pair[1]) / norm

    def sent(ref, sem):
        copy_to(ref, ref, sem, one_r.at[0], other).wait_send()

    for d in range(4):
        sent(sp_in.at[0:64], pair_s.at[d])
    sent(rs_in, one_s.at[0])
    sent(s_full.at[0:240], one_s.at[1])
    sent(u_in, one_s.at[2])
    sent(u_all.at[0:15], one_s.at[3])
    sent(m_z, one_s.at[4])
    sent(u_full.at[0:240], one_s.at[5])
    sent(m_plane.at[0:15], one_s.at[6])
    sent(e_z, one_s.at[7])
    sent(e_plane.at[0:15], one_s.at[8])
    sent(kept, fwd_s.at[0])
    sent(u_kept, fwd_s.at[1])
    sent(m_pair.at[0], fwd_s.at[2])
    sent(e_pair.at[0], fwd_s.at[3])
    for h in range(NSUB):
        for s in range(7):
            sent(t_right.at[s, :, sub(h)], tr_s.at[s, h])
            sent(t_right.at[s, :, sub(h)], gr_s.at[s, h])
        for s in range(8):
            sent(t_left.at[s, :, sub(h)], tl_s.at[s, h])
            sent(t_left.at[s, :, sub(h)], gl_s.at[s, h])
    out_copy.wait()


def shards(right_side, theta_left, theta_right, query_rows, query_cols):
    vmem = pl.BlockSpec(memory_space=pltpu.VMEM)
    dma = pltpu.SemaphoreType.DMA
    residual, answers, ratio = pl.pallas_call(
        kernel,
        out_shape=(
            jax.ShapeDtypeStruct((ROWS, COLS), F32),
            jax.ShapeDtypeStruct((1, NQ), F32),
            jax.ShapeDtypeStruct((1, 128), F32),
        ),
        in_specs=[vmem] * 5,
        out_specs=(pl.BlockSpec(memory_space=pl.ANY), vmem, vmem),
        scratch_shapes=[
            pltpu.VMEM((ROWS, Q), BF16),
            pltpu.VMEM((COLS, NQ), BF16),
            pltpu.VMEM((Q, ROWS), F32),
            pltpu.VMEM((256, ROWS), F32),
            pltpu.VMEM((15, 16, ROWS), F32),
            pltpu.VMEM((Q, ROWS), F32),
            pltpu.VMEM((Q, COLS), F32),
            pltpu.VMEM((7, 32, COLS), F32),
            pltpu.VMEM((8, 32, COLS), F32),
            pltpu.VMEM((Q, COLS), F32),
            pltpu.VMEM((NZ, 1, Q), F32),
            pltpu.VMEM((15, 1, Q), F32),
            pltpu.VMEM((NZ, 1, Q), F32),
            pltpu.VMEM((NZ, Q), F32),
            pltpu.VMEM((Q, Q), F32),
            pltpu.VMEM((ROWS, COLS), F32),
            pltpu.VMEM((ROWS, COLS), F32),
            pltpu.VMEM((Q, COLS), BF16),
            pltpu.VMEM((Q, COLS), BF16),
            pltpu.VMEM((1, MSG), F32),
            pltpu.VMEM((15, 1, MSG), F32),
            pltpu.VMEM((16, 1, MSG), F32),
            pltpu.VMEM((2, 1, MSG), F32),
            pltpu.VMEM((1, 128), F32),
            pltpu.VMEM((15, 1, 128), F32),
            pltpu.VMEM((16, 1, 128), F32),
            pltpu.VMEM((2, 1, 128), F32),
            dma((4,)), dma((4,)),
            dma((9,)), dma((9,)),
            dma((4,)), dma((4,)),
            dma((7, NSUB)), dma((7, NSUB)),
            dma((8, NSUB)), dma((8, NSUB)),
            dma((7, NSUB)), dma((7, NSUB)),
            dma((8, NSUB)), dma((8, NSUB)),
            dma,
        ],
        compiler_params=pltpu.CompilerParams(
            collective_id=0, has_side_effects=True, vmem_limit_bytes=48 * 1024 * 1024
        ),
        name="step",
    )(right_side, theta_left, theta_right, query_rows.T, query_cols.T)
    return residual, ratio[0, 0:1], answers.reshape(NQ)


def solution(mesh):
    return jax.shard_map(
        shards,
        mesh=mesh,
        in_specs=(P("row", "col"), P(None, "row"), P(None, "col"), P(), P()),
        out_specs=(P("row", "col"), P(), P()),
        check_vma=False,
    )
```

time: 612 us -> 101 us (0.17)
  waiting for transfers between devices: 270 us -> 0 us
  blocking collectives: 262 us -> 0 us
  Pallas kernels: 0 us -> 91.7 us
  local copies, waits for them, and re-layouts: 30.8 us -> 6.79 us
  matrix products: 19.9 us -> 0 us
  between operations: 18.2 us -> 1.82 us
  other arithmetic: 10.5 us -> 0 us
    psum x2 -> x0, waiting for transfers between devices: 270 us -> none  [the longest x1 144 us: shards(): summed_right = lax.psum(partial_right, 'col')]
    psum x2 -> x0, blocking collectives: 218 us -> none  [the longest x1 111 us: shards(): start_norm = lax.psum(jnp.sum(start_field * start_field), ('row', 'col'))]
    pallas_call x0 -> x1, Pallas kernels: none -> 91.7 us  [shards(): pl.pallas_call(kernel, out_shape=(jax.ShapeDtypeStruct((ROWS, COLS), F32)...]
    all_gather x2 -> x0, blocking collectives: 44.4 us -> none  [prefix_2(): gathered = lax.all_gather(part, axis)]
    gather x4 -> x0, local copies, waits for them, and re-layouts: 24.6 us -> none  [corner_value(): return jnp.where(inside, jnp.take(flat_prefix, position_flat), 0.0)]
    dot_general x6 -> x0, matrix products: 19.9 us -> none  [the longest x1 5.48 us: shards(): lax.dot_general(left_wide, summed_left, (((0,), (0,)), ((), ())), precisi...]
  transfers between devices with their start and end apart: 2 -> 0, of which waited for: 2 -> 0; matrix products, arithmetic and copies ran while one was open for 1% -> 0% of each run, Pallas kernels for 0% -> 0%
where the time goes in v1:
time: 101 us; the launch traced here: 100 us
  Pallas kernels  91.7 us (91%)
  local copies, waits for them, and re-layouts  6.79 us (7%)
  between operations  1.82 us (2%)
    pallas_call x1, Pallas kernels, shards(): pl.pallas_call(kernel, out_shape=(jax.ShapeDtypeStruct((ROWS, COLS), F32)...  91.7 us
    unnamed x12, local copies, waits for them, and re-layouts  6.79 us

profile of v1, /device:TPU:1, one launch (start us, length us, event | category | flops | bytes accessed | tf_op | source)
XLA Modules:
  0.0 100.3 jit_solution(12459747833138402538)
XLA Ops:
  0.6 0.0 copy-start
  0.6 1.2 %copy-done = bf16[1024,512]{1,0:T(8,128)(2,1)S(1)} copy-done((bf16[1024,512]{1,0:T(8,128)(2,1)S(1)}, bf16[1024,512]{1,0:T(8,128)(2,1)}, u32[]{:S(2)}) %copy-start) | copy-done | bytes 1048600
  1.9 0.0 copy-start.1
  1.9 1.2 %copy-done.1 = bf16[512,1024]{1,0:T(8,128)(2,1)S(1)} copy-done((bf16[512,1024]{1,0:T(8,128)(2,1)S(1)}, bf16[512,1024]{1,0:T(8,128)(2,1)}, u32[]{:S(2)}) %copy-start.1) | copy-done | bytes 1048600
  3.1 0.0 copy-start.2
  3.1 1.0 %copy-done.2 = bf16[512,512]{1,0:T(8,128)(2,1)S(1)} copy-done((bf16[512,512]{1,0:T(8,128)(2,1)S(1)}, bf16[512,512]{1,0:T(8,128)(2,1)}, u32[]{:S(2)}) %copy-start.2) | copy-done | bytes 524312
  4.1 0.0 copy-start.3
  4.1 0.7 copy-done.3
  4.8 0.0 copy-start.4
  4.8 0.7 copy-done.4
  5.5 91.7 %step.1 = (f32[1024,512]{1,0:T(8,128)S(1)}, f32[1,1024]{1,0:T(1,128)S(1)}, f32[1,128]{1,0:T(1,128)S(1)}) custom-call(bf16[1024,512]{1,0:T(8,128)(2,1)S(1)} %copy-done, bf16[512,1024]{1,0:T(8,128)(2,1)S(1)} %copy-done.1, bf16[512,512]{1,0:T(8,128)(2,1)S(1)} %copy-done.2, s32[2,1024]{1,0:T(2,128)S(1)} %bitcast.5, s32[2,1024]{1,0:T(2,128)S(1)} %bitcast.6), custom_call_target="tpu_custom_call" | custom-call | tf_op jit(solution)/shard_map/step/pallas_call | solution.py:423
  97.2 1.3 %copy.11 = f32[1024,512]{1,0:T(8,128)} copy(f32[1024,512]{1,0:T(8,128)S(1)} %get-tuple-element.12) | data formatting | bytes 4194304
  98.6 0.6 copy.13
Async XLA Ops:
  0.6 1.2 %copy-start = (bf16[1024,512]{1,0:T(8,128)(2,1)S(1)}, bf16[1024,512]{1,0:T(8,128)(2,1)}, u32[]{:S(2)}) copy-start(bf16[1024,512]{1,0:T(8,128)(2,1)} %v_ref.1) | copy-start | bytes 3145732
  1.9 1.2 %copy-start.1 = (bf16[512,1024]{1,0:T(8,128)(2,1)S(1)}, bf16[512,1024]{1,0:T(8,128)(2,1)}, u32[]{:S(2)}) copy-start(bf16[512,1024]{1,0:T(8,128)(2,1)} %l_ref.1) | copy-start | bytes 3145732
  3.1 1.0 %copy-start.2 = (bf16[512,512]{1,0:T(8,128)(2,1)S(1)}, bf16[512,512]{1,0:T(8,128)(2,1)}, u32[]{:S(2)}) copy-start(bf16[512,512]{1,0:T(8,128)(2,1)} %r_ref.1) | copy-start | bytes 1572868
  4.1 0.7 copy-start.3
  4.8 0.7 copy-start.4

commit v2 on v1

v2 whole, which is shorter than its diff:
```python
import functools

import jax
import jax.numpy as jnp
from jax import lax
from jax.experimental import pallas as pl
from jax.experimental.pallas import tpu as pltpu
from jax.sharding import PartitionSpec as P

MESH = pl.DeviceIdType.MESH
F32, BF16 = jnp.float32, jnp.bfloat16
NZ, NX, NY = 16, 4, 4
ROWS, COLS, Q, NQ = 1024, 512, 512, 1024
NSUB = 1
JUMP = 5
SUBW = COLS // NSUB
NT = (((1,), (1,)), ((), ()))


def dot(a, b):
    return jnp.dot(a, b, preferred_element_type=F32)


def split(value):
    high = value.astype(BF16)
    return high, (value - high.astype(F32)).astype(BF16)


def dot_split(value, b):
    high, low = split(value)
    return dot(high, b) + dot(low, b)


def copy_to(src, dst, send, recv, device):
    return pltpu.make_async_remote_copy(
        src_ref=src, dst_ref=dst, send_sem=send, recv_sem=recv, device_id=device, device_id_type=MESH
    )


def kernel(
    v_hbm, l_hbm, r_hbm, qr_ref, qc_ref,
    out_ref, ans_ref, ratio_ref,
    v_ref, l_ref, r_ref,
    lt, bt, sp, sp_in, a_in, b_in, a_sum, b_sum, a2_in, b2_in, s_full,
    tp, t_near_r, t_near_l, t_far_r, t_far_l, t_full, u_out, u_in, u_all, u_tile, u_full, ur,
    x1, resid, z_hi, z_lo, m_out, m_z, m_plane, m_pair, e_z, e_plane, e_pair,
    pair_s, pair_r, one_s, one_r, grp_r, fwd_s, fwd_r, tr_s, tr_r, gr_s, gr_r, in_sem, out_sem,
):
    z = lax.axis_index("row")
    c = lax.axis_index("col")
    core = lax.rem(c, 2)
    chip = c // 2
    xx = lax.rem(chip, NX)
    yy = chip // NX

    def z_peer(d):
        return (lax.rem(z + d, NZ), c)

    def plane_chip(j):
        return lax.rem(yy + j // NX, NY) * NX + lax.rem(xx + lax.rem(j, NX), NX)

    def plane_peer(j):
        return (z, plane_chip(j) * 2 + core)

    def x_peer(d):
        return (z, (yy * NX + lax.rem(xx + d, NX)) * 2 + core)

    def y_peer(d):
        return (z, (lax.rem(yy + d, NY) * NX + xx) * 2 + core)

    other = (z, chip * 2 + 1 - core)
    right, left = z_peer(1), z_peer(NZ - 1)

    loads = [
        pltpu.make_async_copy(src, dst, in_sem.at[i])
        for i, (src, dst) in enumerate(((r_hbm, r_ref), (v_hbm, v_ref), (l_hbm, l_ref)))
    ]
    for load in loads:
        load.start()
    barrier = pltpu.get_barrier_semaphore()

    def greet(d, carry):
        pl.semaphore_signal(barrier, inc=1, device_id=z_peer(d), device_id_type=MESH)
        pl.semaphore_signal(barrier, inc=1, device_id=plane_peer(d), device_id_type=MESH)
        return carry

    pl.semaphore_signal(barrier, inc=1, device_id=other, device_id_type=MESH)
    lax.fori_loop(1, NZ, greet, 0)

    def s_half(half):
        rows = pl.ds(pl.multiple_of(half * 256, 256), 256)

        def tile(i, carry):
            at = pl.multiple_of(i * 256, 256)
            block = lax.dot_general(r_ref[rows, :], v_ref[pl.ds(at, 256), :], NT, preferred_element_type=F32)
            sp[half, :, :, :, :, pl.ds(at, 256)] = block.reshape(NY, NX, 2, 8, 256)
            return carry

        lax.fori_loop(0, 4, tile, 0)

    def t_tile(i, carry):
        at = pl.multiple_of(i * 256, 256)
        tp[pl.ds(at, 256), :] = dot(l_ref[pl.ds(at, 256), :], v_ref[...])
        return carry

    loads[0].wait()
    loads[1].wait()
    s_half(1 - core)
    pl.semaphore_wait(barrier, 31)

    give, keep = (1 - core) * 256, core * 256
    order = (2, 1, 3, 0)

    def x_at(d):
        return lax.rem(xx + d, NX)

    def y_at(d):
        return lax.rem(yy + d, NY)

    def pair_a(d):
        return copy_to(
            sp.at[1 - core, :, x_at(d), 0], sp_in.at[:, x_at(d), 0], pair_s.at[0, d], pair_r.at[0, d], other
        )

    def pair_b(d):
        return copy_to(
            sp.at[1 - core, y_at(d), :, 1], sp_in.at[y_at(d), :, 1], pair_s.at[1, d], pair_r.at[1, d], other
        )

    for d in order:
        pair_a(d).start()
        pair_b(d).start()

    def t_rows(block):
        return pl.ds(pl.multiple_of(lax.rem(block + 2 * NZ, NZ) * 32, 32), 32)

    def sub(h):
        return pl.ds(h * SUBW, SUBW)

    rs_flows = (
        (1, tuple(range(7, JUMP - 1, -1)), t_far_r, 2, True),
        (-1, tuple(range(8, JUMP - 1, -1)), t_far_l, 3, True),
        (1, tuple(range(JUMP - 1, 0, -1)), t_near_r, 0, False),
        (-1, tuple(range(JUMP - 1, 0, -1)), t_near_l, 1, False),
    )

    def t_dev(offset):
        return z_peer(offset + NZ)

    def t_rs(s):
        k = s - 1
        for h in range(NSUB):
            for sign, dist, buf, f, far in rs_flows:
                if k >= len(dist):
                    continue
                rows = t_rows(z + sign * dist[k])
                src = tp.at[rows, sub(h)]
                if k:
                    src = buf.at[k - 1, :, sub(h)]
                    copy_to(src, src, tr_s.at[f, k - 1, h], tr_r.at[f, k - 1, h], right).wait_recv()
                    buf[k - 1, :, sub(h)] = buf[k - 1, :, sub(h)] + tp[rows, sub(h)]
                hop = JUMP if far and k == len(dist) - 1 else 1
                copy_to(src, buf.at[k, :, sub(h)], tr_s.at[f, k, h], tr_r.at[f, k, h], t_dev(sign * hop)).start()

    def t_own():
        rows = t_rows(z)
        total = jnp.zeros((1, SUBW), F32)
        for h in range(NSUB):
            block = tp[rows, sub(h)]
            for sign, dist, buf, f, far in rs_flows:
                last = len(dist) - 1
                here = buf.at[last, :, sub(h)]
                copy_to(here, here, tr_s.at[f, last, h], tr_r.at[f, last, h], right).wait_recv()
                block = block + buf[last, :, sub(h)]
            t_full[rows, sub(h)] = block
            total = total + jnp.sum(block * block, axis=0, keepdims=True)
        return jnp.sum(total)

    def t_ag(s, far_flows):
        k = s - 1
        for h in range(NSUB):
            for sign, dist, buf, f, far in rs_flows:
                n = len(dist)
                if k > n or far != far_flows:
                    continue
                offset = 0 if k == 0 else sign * (k + JUMP - 1 if far else k)
                here = t_full.at[t_rows(z - offset), sub(h)]
                if k:
                    copy_to(here, here, gr_s.at[f, k - 1, h], gr_r.at[f, k - 1, h], right).wait_recv()
                if k < n:
                    hop = JUMP if far and k == 0 else 1
                    copy_to(here, here, gr_s.at[f, k, h], gr_r.at[f, k, h], t_dev(sign * hop)).start()

    def near(s):
        t_ag(s, False)

    def far(s):
        t_ag(s, True)

    loads[2].wait()
    lax.fori_loop(0, 2, t_tile, 0)
    t_rs(1)
    s_half(core)

    for d in order:
        pair_a(d).wait_recv()
        x_to = x_at(d)
        sp[core, :, x_to, 0] = sp[core, :, x_to, 0] + sp_in[:, x_to, 0]
        if d:
            src = sp.at[core, :, x_to, 0]
            copy_to(src, a_in.at[d - 1], one_s.at[0], one_r.at[0], x_peer(d)).start()
        pair_b(d).wait_recv()
        y_to = y_at(d)
        sp[core, y_to, :, 1] = sp[core, y_to, :, 1] + sp_in[y_to, :, 1]
        if d:
            src = sp.at[core, y_to, :, 1]
            copy_to(src, b_in.at[d - 1], one_s.at[1], one_r.at[1], y_peer(d)).start()

    def lt_tile(i, carry):
        at = pl.multiple_of(i * 128, 128)
        lt[pl.ds(at, 128), :] = l_ref[:, pl.ds(at, 128)].astype(F32).T.astype(BF16)
        return carry

    def bt_tile(i, carry):
        at = pl.multiple_of(i * 128, 128)
        index = lax.broadcasted_iota(jnp.int32, (128, NQ), 0) + (at + c * COLS)
        inside = (index >= qc_ref[0:1, :]) & (index < qc_ref[1:2, :])
        bt[pl.ds(at, 128), :] = jnp.where(inside, 1.0, 0.0).astype(BF16)
        return carry

    def answer_tile(i, carry):
        total, norm = carry
        at = pl.multiple_of(i * 256, 256)
        block = v_ref[pl.ds(at, 256), :]
        across = dot(block, bt[...])
        index = lax.broadcasted_iota(jnp.int32, (256, NQ), 0) + (at + z * ROWS)
        inside = (index >= qr_ref[0:1, :]) & (index < qr_ref[1:2, :])
        total = total + jnp.sum(jnp.where(inside, across, 0.0), axis=0, keepdims=True)
        wide = block.astype(F32)
        norm = norm + jnp.sum(wide * wide, axis=0, keepdims=True)
        return total, norm

    def chips_row(base, d):
        return pl.ds(pl.multiple_of(base + lax.rem(yy + NY - d, NY) * 64, 64), 64)

    def forward(full, f, d):
        got = full.at[pl.ds(0, 64 if d else 48)]
        copy_to(got, got, fwd_s.at[f, d], grp_r.at[f, d], other).wait_recv()
        here = full.at[chips_row(keep, d)]
        copy_to(here, here, fwd_s.at[f, d], fwd_r.at[f, d], other).start()

    def forwarded(full, f):
        for d in (0, 1, 3, 2):
            here = full.at[chips_row(give, d)]
            copy_to(here, here, fwd_s.at[f, d], fwd_r.at[f, d], other).wait_recv()

    def x_part(half, first):
        rows = pl.ds(pl.multiple_of(half * 256, 256), 256)

        def tile(i, carry):
            at = pl.multiple_of(i * 256, 256)
            high, low = split(s_full[rows, pl.ds(at, 256)].T)
            have = v_ref[pl.ds(at, 256), :].astype(F32) if first else x1[pl.ds(at, 256), :]
            x1[pl.ds(at, 256), :] = have + dot(high, r_ref[rows, :]) + dot(low, r_ref[rows, :])
            return carry

        lax.fori_loop(0, 4, tile, 0)

    def u_part_of(half):
        rows = pl.ds(pl.multiple_of(half * 256, 256), 256)
        high, low = split(u_full[rows, :].T)
        return dot(high, r_ref[rows, :]) + dot(low, r_ref[rows, :])

    t_rs(2)
    lax.fori_loop(0, 8, lt_tile, 0)
    copy_to(a_in, a_in, one_s.at[0], one_r.at[0], other).wait_recv()
    for d in (2, 1, 3):
        y_to = y_at(d)
        a_sum[d - 1] = sp[core, y_to, xx, 0] + a_in[0, y_to] + a_in[1, y_to] + a_in[2, y_to]
        copy_to(a_sum.at[d - 1], a2_in.at[d - 1], one_s.at[2], one_r.at[2], y_peer(d)).start()
    copy_to(b_in, b_in, one_s.at[1], one_r.at[1], other).wait_recv()
    for d in (2, 1, 3):
        x_to = x_at(d)
        b_sum[d - 1] = sp[core, yy, x_to, 1] + b_in[0, x_to] + b_in[1, x_to] + b_in[2, x_to]
        copy_to(b_sum.at[d - 1], b2_in.at[d - 1], one_s.at[3], one_r.at[3], x_peer(d)).start()
    t_rs(3)
    lax.fori_loop(0, 4, bt_tile, 0)
    own_rows = pl.ds(pl.multiple_of(keep + chip * 16, 16), 16)
    s_a = sp[core, yy, xx, 0] + a_in[0, yy] + a_in[1, yy] + a_in[2, yy]
    s_b = sp[core, yy, xx, 1] + b_in[0, xx] + b_in[1, xx] + b_in[2, xx]
    copy_to(a2_in, a2_in, one_s.at[2], one_r.at[2], other).wait_recv()
    copy_to(b2_in, b2_in, one_s.at[3], one_r.at[3], other).wait_recv()
    s_a = s_a + a2_in[0] + a2_in[1] + a2_in[2]
    s_b = s_b + b2_in[0] + b2_in[1] + b2_in[2]
    s_block = jnp.concatenate([s_a, s_b], axis=0)
    s_full[own_rows, :] = s_block

    def group(j):
        return j // NX

    def s_copy(j):
        here = s_full.at[own_rows]
        return copy_to(here, here, one_s.at[4], grp_r.at[0, group(j)], plane_peer(j))

    def start_all(make):
        def one(j, carry):
            make(j).start()
            return carry

        lax.fori_loop(1, 16, one, 0)

    def start_far(make):
        make(8).start()

        def one(j, carry):
            make(8 - j).start()
            make(8 + j).start()
            return carry

        lax.fori_loop(1, 8, one, 0)

    s_high, s_low = split(s_block)
    u_part = lax.dot_general(s_high, l_ref[...], NT, preferred_element_type=F32) + lax.dot_general(
        s_low, l_ref[...], NT, preferred_element_type=F32
    )
    for i in range(NZ):
        u_out[i] = u_part[i : i + 1, :]

    def u_copy(d):
        return copy_to(u_out.at[lax.rem(z + d, NZ)], u_in.at[d - 1], one_s.at[5], one_r.at[5], z_peer(d))

    start_far(u_copy)
    start_all(s_copy)
    t_rs(4)
    carry = (jnp.zeros((1, NQ), F32), jnp.zeros((1, COLS), F32))
    carry = lax.fori_loop(0, 4, answer_tile, carry)
    copy_to(u_in, u_in, one_s.at[5], one_r.at[5], other).wait_recv()

    def add_row(j, total):
        return total + u_in[j]

    u_row = lax.fori_loop(0, 15, add_row, u_out[z])
    u_all[z] = u_row

    def ug_copy(d):
        return copy_to(u_all.at[z], u_all.at[z], one_s.at[6], one_r.at[6], z_peer(d))

    start_far(ug_copy)
    t_norm = t_own()
    far(1)
    near(1)
    rest = jnp.sum(s_block * s_block) + jnp.sum(u_row * u_row) + t_norm
    lane = lax.broadcasted_iota(jnp.int32, (1, 128), 1)
    for g in range(8):
        m_out[g, :, 0:128] = carry[0][:, g * 128 : g * 128 + 128]
        m_out[g, :, 128:256] = jnp.where(lane < 64, jnp.sum(carry[1]), rest)

    def eighth(d):
        return lax.rem(z + d, 8)

    def m_copy(d):
        return copy_to(m_out.at[eighth(d)], m_z.at[d - 1], one_s.at[7], one_r.at[7], z_peer(d))

    start_far(m_copy)

    near(2)
    far(2)
    for d in (0, 1, 3, 2):
        forward(s_full, 0, d)
    copy_to(u_all.at[0:15], u_all.at[0:15], one_s.at[6], one_r.at[6], other).wait_recv()
    for i in range(NZ):
        u_tile[i : i + 1, :] = u_all[i]
    u_full[own_rows, :] = u_tile[...]

    def up_copy(j):
        here = u_full.at[own_rows]
        return copy_to(here, here, one_s.at[8], grp_r.at[1, group(j)], plane_peer(j))

    start_all(up_copy)
    near(3)
    far(3)
    x_part(core, True)
    copy_to(m_z, m_z, one_s.at[7], one_r.at[7], other).wait_recv()

    def add_m(buffer):
        return lambda j, total: total + buffer[j]

    m_plane[15] = lax.fori_loop(0, 15, add_m(m_z), m_out[eighth(0)])

    def mp_copy(j):
        return copy_to(m_plane.at[15], m_plane.at[j - 1], one_s.at[9], one_r.at[9], plane_peer(j))

    start_all(mp_copy)
    near(4)
    far(4)
    forwarded(s_full, 0)
    x_part(1 - core, False)
    for d in (0, 1, 3, 2):
        forward(u_full, 1, d)
    copy_to(m_plane.at[0:15], m_plane.at[0:15], one_s.at[9], one_r.at[9], other).wait_recv()
    m_pair[0] = lax.fori_loop(0, 16, add_m(m_plane), jnp.zeros((1, 256), F32))
    m_copy_pair = copy_to(m_pair.at[0], m_pair.at[1], one_s.at[12], one_r.at[12], other)
    m_copy_pair.start()
    ur[...] = u_part_of(core)
    forwarded(u_full, 1)
    ur[...] = ur[...] + u_part_of(1 - core)
    near(5)
    far(5)
    m_copy_pair.wait_recv()
    message = m_pair[0] + m_pair[1]
    norm = message[0:1, 128:129]
    alpha = norm / (norm + message[0:1, 192:193])
    high, low = split(t_full[...] + ur[...])
    z_hi[...] = high
    z_lo[...] = low

    def final_tile(i, total):
        at = pl.multiple_of(i * 256, 256)
        rows = lt[pl.ds(at, 256), :]
        image = x1[pl.ds(at, 256), :] + dot(rows, z_hi[...]) + dot(rows, z_lo[...])
        block = v_ref[pl.ds(at, 256), :].astype(F32) - alpha * image
        resid[pl.ds(at, 256), :] = block
        return total + jnp.sum(block * block, axis=0, keepdims=True)

    fresh = lax.fori_loop(0, 4, final_tile, jnp.zeros((1, COLS), F32))
    out_copy = pltpu.make_async_copy(resid, out_ref, out_sem)
    out_copy.start()

    e_z[15, :, 0:128] = jnp.broadcast_to(jnp.sum(fresh), (1, 128))
    e_z[15, :, 128:256] = message[:, 0:128]

    def ez_copy(d):
        return copy_to(e_z.at[15], e_z.at[d - 1], one_s.at[10], one_r.at[10], z_peer(d))

    start_far(ez_copy)
    copy_to(e_z.at[0:15], e_z.at[0:15], one_s.at[10], one_r.at[10], other).wait_recv()
    e_plane[15] = lax.fori_loop(0, 16, add_m(e_z), jnp.zeros((1, 256), F32))

    def ep_copy(j):
        return copy_to(e_plane.at[15], e_plane.at[j - 1], one_s.at[11], one_r.at[11], plane_peer(j))

    start_all(ep_copy)
    spans = (qr_ref[1:2, :] - qr_ref[0:1, :]).astype(F32) * (qc_ref[1:2, :] - qc_ref[0:1, :]).astype(F32)
    scale = alpha / jnp.sqrt(spans)
    for g in range(8):
        slot = lax.rem(z - g - 1 + 2 * NZ, NZ)
        part = slice(g * 128, g * 128 + 128)
        ans_ref[:, part] = e_z[slot, :, 128:256] * scale[:, part]
    copy_to(e_plane.at[0:15], e_plane.at[0:15], one_s.at[11], one_r.at[11], other).wait_recv()
    e_pair[0] = lax.fori_loop(0, 16, add_m(e_plane), jnp.zeros((1, 256), F32))
    e_copy_pair = copy_to(e_pair.at[0], e_pair.at[1], one_s.at[13], one_r.at[13], other)
    e_copy_pair.start()
    e_copy_pair.wait_recv()
    total = e_pair[0] + e_pair[1]
    ratio_ref[...] = total[:, 0:128] / norm

    def sent(ref, sem):
        copy_to(ref, ref, sem, one_r.at[0], other).wait_send()

    for d in range(4):
        sent(sp_in.at[:, 0, 0], pair_s.at[0, d])
        sent(sp_in.at[0, :, 1], pair_s.at[1, d])
        sent(s_full.at[0:64], fwd_s.at[0, d])
        sent(u_full.at[0:64], fwd_s.at[1, d])
    sent(a_in, one_s.at[0])
    sent(b_in, one_s.at[1])
    sent(a2_in, one_s.at[2])
    sent(b2_in, one_s.at[3])
    sent(s_full.at[0:240], one_s.at[4])
    sent(u_in, one_s.at[5])
    sent(u_all.at[0:15], one_s.at[6])
    sent(m_z, one_s.at[7])
    sent(u_full.at[0:240], one_s.at[8])
    sent(m_plane.at[0:15], one_s.at[9])
    sent(e_z.at[0:15], one_s.at[10])
    sent(e_plane.at[0:15], one_s.at[11])
    sent(m_pair.at[0], one_s.at[12])
    sent(e_pair.at[0], one_s.at[13])
    for sign, dist, buf, f, far in rs_flows:
        for k in range(len(dist)):
            for h in range(NSUB):
                sent(buf.at[k, :, sub(h)], tr_s.at[f, k, h])
                sent(buf.at[k, :, sub(h)], gr_s.at[f, k, h])
    out_copy.wait()


def shards(right_side, theta_left, theta_right, query_rows, query_cols):
    vmem = pl.BlockSpec(memory_space=pltpu.VMEM)
    hbm = pl.BlockSpec(memory_space=pltpu.HBM)
    dma = pltpu.SemaphoreType.DMA
    residual, answers, ratio = pl.pallas_call(
        kernel,
        out_shape=(
            jax.ShapeDtypeStruct((ROWS, COLS), F32),
            jax.ShapeDtypeStruct((1, NQ), F32),
            jax.ShapeDtypeStruct((1, 128), F32),
        ),
        in_specs=[hbm] * 3 + [vmem] * 2,
        out_specs=(hbm, vmem, vmem),
        scratch_shapes=[
            pltpu.VMEM((ROWS, COLS), BF16),
            pltpu.VMEM((Q, ROWS), BF16),
            pltpu.VMEM((Q, COLS), BF16),
            pltpu.VMEM((ROWS, Q), BF16),
            pltpu.VMEM((COLS, NQ), BF16),
            pltpu.VMEM((2, NY, NX, 2, 8, ROWS), F32),
            pltpu.VMEM((NY, NX, 2, 8, ROWS), F32),
            pltpu.VMEM((3, NY, 8, ROWS), F32),
            pltpu.VMEM((3, NX, 8, ROWS), F32),
            pltpu.VMEM((3, 8, ROWS), F32),
            pltpu.VMEM((3, 8, ROWS), F32),
            pltpu.VMEM((3, 8, ROWS), F32),
            pltpu.VMEM((3, 8, ROWS), F32),
            pltpu.VMEM((Q, ROWS), F32),
            pltpu.VMEM((Q, COLS), F32),
            pltpu.VMEM((JUMP - 1, 32, COLS), F32),
            pltpu.VMEM((JUMP - 1, 32, COLS), F32),
            pltpu.VMEM((8 - JUMP, 32, COLS), F32),
            pltpu.VMEM((9 - JUMP, 32, COLS), F32),
            pltpu.VMEM((Q, COLS), F32),
            pltpu.VMEM((NZ, 1, Q), F32),
            pltpu.VMEM((15, 1, Q), F32),
            pltpu.VMEM((NZ, 1, Q), F32),
            pltpu.VMEM((NZ, Q), F32),
            pltpu.VMEM((Q, Q), F32),
            pltpu.VMEM((Q, COLS), F32),
            pltpu.VMEM((ROWS, COLS), F32),
            pltpu.VMEM((ROWS, COLS), F32),
            pltpu.VMEM((Q, COLS), BF16),
            pltpu.VMEM((Q, COLS), BF16),
            pltpu.VMEM((8, 1, 256), F32),
            pltpu.VMEM((15, 1, 256), F32),
            pltpu.VMEM((16, 1, 256), F32),
            pltpu.VMEM((2, 1, 256), F32),
            pltpu.VMEM((16, 1, 256), F32),
            pltpu.VMEM((16, 1, 256), F32),
            pltpu.VMEM((2, 1, 256), F32),
            dma((2, 4)), dma((2, 4)),
            dma((14,)), dma((14,)),
            dma((2, 4)),
            dma((2, 4)), dma((2, 4)),
            dma((4, 8, NSUB)), dma((4, 8, NSUB)),
            dma((4, 8, NSUB)), dma((4, 8, NSUB)),
            dma((3,)),
            dma,
        ],
        compiler_params=pltpu.CompilerParams(
            collective_id=0, has_side_effects=True, vmem_limit_bytes=60 * 1024 * 1024
        ),
        name="step",
    )(right_side, theta_left, theta_right, query_rows.T, query_cols.T)
    return residual, ratio[0, 0:1], answers.reshape(NQ)


def solution(mesh):
    return jax.shard_map(
        shards,
        mesh=mesh,
        in_specs=(P("row", "col"), P(None, "row"), P(None, "col"), P(), P()),
        out_specs=(P("row", "col"), P(), P()),
        check_vma=False,
    )
```

time: 101 us -> 90.9 us (0.900)
  Pallas kernels: 91.7 us -> 85.1 us
  local copies, waits for them, and re-layouts: 6.79 us -> 3.68 us
    pallas_call x1, Pallas kernels: 91.7 us -> 85.1 us  [shards(): pl.pallas_call(kernel, out_shape=(jax.ShapeDtypeStruct((ROWS, COLS), F32)...]
    unnamed x12 -> x6, local copies, waits for them, and re-layouts: 6.79 us -> 3.68 us
where the time goes in v2:
time: 90.9 us; the launch traced here: 90.7 us
  Pallas kernels  85.1 us (94%)
  local copies, waits for them, and re-layouts  3.68 us (4%)
  between operations  1.83 us (2%)
    pallas_call x1, Pallas kernels, shards(): pl.pallas_call(kernel, out_shape=(jax.ShapeDtypeStruct((ROWS, COLS), F32)...  85.1 us
    unnamed x6, local copies, waits for them, and re-layouts  3.68 us

profile of v2, /device:TPU:1, one launch (start us, length us, event | category | flops | bytes accessed | tf_op | source)
XLA Modules:
  0.0 90.7 jit_solution(12863891441937833438)
XLA Ops:
  0.6 85.1 %step.1 = (f32[1024,512]{1,0:T(8,128)}, f32[1,1024]{1,0:T(1,128)}, f32[1,128]{1,0:T(1,128)}) custom-call(bf16[1024,512]{1,0:T(8,128)(2,1)} %v_hbm.1, bf16[512,1024]{1,0:T(8,128)(2,1)} %l_hbm.1, bf16[512,512]{1,0:T(8,128)(2,1)} %r_hbm.1, s32[2,1024]{1,0:T(2,128)} %bitcast.5, s32[2,1024]{1,0:T(2,128)} %bitcast.6), custom_call_target="tpu_custom_call" | custom-call | tf_op jit(solution)/shard_map/step/pallas_call | solution.py:491
  85.8 0.0 copy-start.1
  85.8 0.0 copy-start
  85.8 3.1 %copy.11 = f32[1024,512]{1,0:T(8,128)} copy(f32[1024,512]{1,0:T(8,128)} %get-tuple-element.12) | data formatting | bytes 4194304
  88.9 0.0 copy-done.1
  88.9 0.0 copy-done
  88.9 0.6 copy.13
Async XLA Ops:
  85.8 3.1 %copy-start.1 = (f32[1,128]{1,0:T(1,128)S(1)}, f32[1,128]{1,0:T(1,128)}, u32[]{:S(2)}) copy-start(f32[1,128]{1,0:T(1,128)} %get-tuple-element.7) | copy-start | bytes 1540
  85.8 3.1 %copy-start = (f32[1,1024]{1,0:T(1,128)S(1)}, f32[1,1024]{1,0:T(1,128)}, u32[]{:S(2)}) copy-start(f32[1,1024]{1,0:T(1,128)} %get-tuple-element.8) | copy-start | bytes 12292

commit v3 on v2

--- a/solution.py
+++ b/solution.py
@@ -13,6 +13,7 @@
 ROWS, COLS, Q, NQ = 1024, 512, 512, 1024
 NSUB = 1
 JUMP = 5
+GATHER = 5
 SUBW = COLS // NSUB
 NT = (((1,), (1,)), ((), ()))
 
@@ -176,19 +177,22 @@
             total = total + jnp.sum(block * block, axis=0, keepdims=True)
         return jnp.sum(total)
 
+    def ag_count(sign, far):
+        return (8 if sign > 0 else 9) - GATHER if far else GATHER - 1
+
     def t_ag(s, far_flows):
         k = s - 1
         for h in range(NSUB):
             for sign, dist, buf, f, far in rs_flows:
-                n = len(dist)
+                n = ag_count(sign, far)
                 if k > n or far != far_flows:
                     continue
-                offset = 0 if k == 0 else sign * (k + JUMP - 1 if far else k)
+                offset = 0 if k == 0 else sign * (k + GATHER - 1 if far else k)
                 here = t_full.at[t_rows(z - offset), sub(h)]
                 if k:
                     copy_to(here, here, gr_s.at[f, k - 1, h], gr_r.at[f, k - 1, h], right).wait_recv()
                 if k < n:
-                    hop = JUMP if far and k == 0 else 1
+                    hop = GATHER if far and k == 0 else 1
                     copy_to(here, here, gr_s.at[f, k, h], gr_r.at[f, k, h], t_dev(sign * hop)).start()
 
     def near(s):
@@ -284,7 +288,6 @@
         b_sum[d - 1] = sp[core, yy, x_to, 1] + b_in[0, x_to] + b_in[1, x_to] + b_in[2, x_to]
         copy_to(b_sum.at[d - 1], b2_in.at[d - 1], one_s.at[3], one_r.at[3], x_peer(d)).start()
     t_rs(3)
-    lax.fori_loop(0, 4, bt_tile, 0)
     own_rows = pl.ds(pl.multiple_of(keep + chip * 16, 16), 16)
     s_a = sp[core, yy, xx, 0] + a_in[0, yy] + a_in[1, yy] + a_in[2, yy]
     s_b = sp[core, yy, xx, 1] + b_in[0, xx] + b_in[1, xx] + b_in[2, xx]
@@ -332,8 +335,6 @@
     start_far(u_copy)
     start_all(s_copy)
     t_rs(4)
-    carry = (jnp.zeros((1, NQ), F32), jnp.zeros((1, COLS), F32))
-    carry = lax.fori_loop(0, 4, answer_tile, carry)
     copy_to(u_in, u_in, one_s.at[5], one_r.at[5], other).wait_recv()
 
     def add_row(j, total):
@@ -349,6 +350,9 @@
     t_norm = t_own()
     far(1)
     near(1)
+    lax.fori_loop(0, 4, bt_tile, 0)
+    carry = (jnp.zeros((1, NQ), F32), jnp.zeros((1, COLS), F32))
+    carry = lax.fori_loop(0, 4, answer_tile, carry)
     rest = jnp.sum(s_block * s_block) + jnp.sum(u_row * u_row) + t_norm
     lane = lax.broadcasted_iota(jnp.int32, (1, 128), 1)
     for g in range(8):
@@ -364,9 +368,6 @@
     start_far(m_copy)
 
     near(2)
-    far(2)
-    for d in (0, 1, 3, 2):
-        forward(s_full, 0, d)
     copy_to(u_all.at[0:15], u_all.at[0:15], one_s.at[6], one_r.at[6], other).wait_recv()
     for i in range(NZ):
         u_tile[i : i + 1, :] = u_all[i]
@@ -377,8 +378,11 @@
         return copy_to(here, here, one_s.at[8], grp_r.at[1, group(j)], plane_peer(j))
 
     start_all(up_copy)
+    far(2)
     near(3)
     far(3)
+    for d in (0, 1, 3, 2):
+        forward(s_full, 0, d)
     x_part(core, True)
     copy_to(m_z, m_z, one_s.at[7], one_r.at[7], other).wait_recv()
 
@@ -477,10 +481,12 @@
     sent(m_pair.at[0], one_s.at[12])
     sent(e_pair.at[0], one_s.at[13])
     for sign, dist, buf, f, far in rs_flows:
+        for k in range(ag_count(sign, far)):
+            for h in range(NSUB):
+                sent(buf.at[0, :, sub(h)], gr_s.at[f, k, h])
         for k in range(len(dist)):
             for h in range(NSUB):
                 sent(buf.at[k, :, sub(h)], tr_s.at[f, k, h])
-                sent(buf.at[k, :, sub(h)], gr_s.at[f, k, h])
     out_copy.wait()
 
 

time: 90.9 us -> 90.9 us (level)
  no operation moved by 1% of the time
where the time goes in v3:
time: 90.9 us; the launch traced here: 90.7 us
  Pallas kernels  85.1 us (94%)
  local copies, waits for them, and re-layouts  3.68 us (4%)
  between operations  1.83 us (2%)
    pallas_call x1, Pallas kernels, shards(): pl.pallas_call(kernel, out_shape=(jax.ShapeDtypeStruct((ROWS, COLS), F32)...  85.1 us
    unnamed x6, local copies, waits for them, and re-layouts  3.68 us

profile of v3, /device:TPU:1, one launch (start us, length us, event | category | flops | bytes accessed | tf_op | source)
XLA Modules:
  0.0 90.7 jit_solution(1017821450707409282)
XLA Ops:
  0.6 85.1 %step.1 = (f32[1024,512]{1,0:T(8,128)}, f32[1,1024]{1,0:T(1,128)}, f32[1,128]{1,0:T(1,128)}) custom-call(bf16[1024,512]{1,0:T(8,128)(2,1)} %v_hbm.1, bf16[512,1024]{1,0:T(8,128)(2,1)} %l_hbm.1, bf16[512,512]{1,0:T(8,128)(2,1)} %r_hbm.1, s32[2,1024]{1,0:T(2,128)} %bitcast.5, s32[2,1024]{1,0:T(2,128)} %bitcast.6), custom_call_target="tpu_custom_call" | custom-call | tf_op jit(solution)/shard_map/step/pallas_call | solution.py:497
  85.8 0.0 copy-start.1
  85.8 0.0 copy-start
  85.8 3.1 %copy.11 = f32[1024,512]{1,0:T(8,128)} copy(f32[1024,512]{1,0:T(8,128)} %get-tuple-element.12) | data formatting | bytes 4194304
  88.9 0.0 copy-done.1
  88.9 0.0 copy-done
  88.9 0.6 copy.13
Async XLA Ops:
  85.8 3.1 %copy-start.1 = (f32[1,128]{1,0:T(1,128)S(1)}, f32[1,128]{1,0:T(1,128)}, u32[]{:S(2)}) copy-start(f32[1,128]{1,0:T(1,128)} %get-tuple-element.7) | copy-start | bytes 1540
  85.8 3.1 %copy-start = (f32[1,1024]{1,0:T(1,128)S(1)}, f32[1,1024]{1,0:T(1,128)}, u32[]{:S(2)}) copy-start(f32[1,1024]{1,0:T(1,128)} %get-tuple-element.8) | copy-start | bytes 12292
